TPU v7x, 128 devices: a whole 4x4x4 slice. The times are simulated.
128 devices in a mesh: lat: 8 (over y_hi, z), lon: 16 (over x, y_lo, core).
Axes of the slice: x: 4, y: 4 (y_hi: 2, y_lo: 2; y = y_hi * 2 + y_lo), z: 4, core: 2. Of those that a mesh axis runs over, the one named last changes fastest.
Arguments:
- fields: bfloat16 [2, 256, 768, 256], P(None, 'lat', 'lon'), may hold values from -6 to 6
- kernel: bfloat16 [9, 256, 256], replicated, may hold values from -0.125 to 0.125
- conv_bias: float32 [256], replicated, may hold values from -3 to 3
- cotangent: bfloat16 [2, 128, 384, 256], P(None, 'lat', 'lon'), may hold values from -6 to 6
Outputs:
- pooled: bfloat16 [2, 128, 384, 256], P(None, 'lat', 'lon')
- grad_input: bfloat16 [2, 256, 768, 256], P(None, 'lat', 'lon')
- grad_kernel: float32 [9, 256, 256], replicated
- grad_bias: float32 [256], replicated
All inputs are finite; a program needn't handle non-finite values.
Results may differ from a plain program's by a relative error of at most 0.013.
Values may be sent and summed in bfloat16 or wider, within the bound.
No kernel may reach another device: no remote copies, remote signals or barrier semaphores. Data moves between devices by JAX's collectives and lax.ppermute only.
A program may use at most 64 MiB of HBM per device.

v0:
```python
import math
import jax
import jax.numpy as jnp
from jax import lax
from jax.sharding import PartitionSpec as P


def shifted(shard, axis, by):
    size = lax.axis_size(axis)
    return lax.ppermute(shard, axis, [(i, (i + by) % size) for i in range(size)])


def with_halo(shard, sides, width, wrap):
    for axis, dim in sides:
        size, length = (lax.axis_size(axis), shard.shape[dim])
        up = [(i, (i + 1) % size) for i in range(size if wrap else size - 1)]
        down = [(j, i) for i, j in up]
        last = lax.slice_in_dim(shard, length - width, length, axis=dim)
        first = lax.slice_in_dim(shard, 0, width, axis=dim)
        before = lax.ppermute(last, axis, up)
        after = lax.ppermute(first, axis, down)
        shard = jnp.concatenate([before, shard, after], axis=dim)
    return shard


def lat_cosine(rows, first, total):
    index_rows = (first + jnp.arange(rows)).astype(jnp.float32)
    return jnp.cos((index_rows + 0.5) * (math.pi / total) - math.pi / 2)


def extend(field):
    lat_count = lax.axis_size("lat")
    lat_place = lax.axis_index("lat")
    lon_count = lax.axis_size("lon")
    north_row = field[:, :1]
    south_row = field[:, -1:]
    mirror_north, mirror_south = shifted((north_row, south_row), "lon", lon_count // 2)
    rim_rows = with_halo(field, (("lat", 1),), 1, False)
    upper_pad = jnp.where(lat_place == 0, mirror_north, rim_rows[:, :1])
    bottom = jnp.where(lat_place == lat_count - 1, mirror_south, rim_rows[:, -1:])
    tall = jnp.concatenate([upper_pad, field, bottom], axis=1)
    return with_halo(tall, (("lon", 2),), 1, True)


def forward_conv(padded, kernel, rows, cols):
    chans = padded.shape[-1]
    total = jnp.zeros((padded.shape[0] * rows * cols, kernel.shape[2]), jnp.float32)
    for row_off in range(3):
        for col_off in range(3):
            window = padded[:, row_off : row_off + rows, col_off : col_off + cols, :].reshape(
                -1, chans
            )
            total = total + jnp.dot(
                window, kernel[3 * row_off + col_off], preferred_element_type=jnp.float32
            )
    return total.reshape(padded.shape[0], rows, cols, kernel.shape[2])


def back_conv(padded, kernel, rows, cols):
    chans = padded.shape[-1]
    total = jnp.zeros((padded.shape[0] * rows * cols, kernel.shape[1]), jnp.float32)
    for row_off in range(3):
        for col_off in range(3):
            window = padded[
                :, 2 - row_off : 2 - row_off + rows, 2 - col_off : 2 - col_off + cols, :
            ].reshape(-1, chans)
            total = total + lax.dot_general(
                window,
                kernel[3 * row_off + col_off],
                (((1,), (1,)), ((), ())),
                preferred_element_type=jnp.float32,
            )
    return total.reshape(padded.shape[0], rows, cols, kernel.shape[1])


def pole_term(pad_row, kernel, row_off, cols):
    chans = pad_row.shape[-1]
    total = jnp.zeros((pad_row.shape[0] * cols, kernel.shape[1]), jnp.float32)
    for col_off in range(3):
        window = pad_row[:, :, 2 - col_off : 2 - col_off + cols, :].reshape(-1, chans)
        total = total + lax.dot_general(
            window,
            kernel[3 * row_off + col_off],
            (((1,), (1,)), ((), ())),
            preferred_element_type=jnp.float32,
        )
    return total.reshape(pad_row.shape[0], 1, cols, kernel.shape[1])


def kernel_grad(padded, grad_pre, rows, cols):
    chans = padded.shape[-1]
    flat_grad = grad_pre.reshape(-1, grad_pre.shape[-1])
    pieces = []
    for row_off in range(3):
        for col_off in range(3):
            window = padded[:, row_off : row_off + rows, col_off : col_off + cols, :].reshape(
                -1, chans
            )
            pieces.append(
                lax.dot_general(
                    window, flat_grad, (((0,), (0,)), ((), ())), preferred_element_type=jnp.float32
                )
            )
    return jnp.stack(pieces, axis=0)


def local(fields, kernel, conv_bias, cotangent):
    batches, rows, cols, chans = fields.shape
    lat_count = lax.axis_size("lat")
    lat_place = lax.axis_index("lat")
    padded = extend(fields)
    pre = forward_conv(padded, kernel, rows, cols) + conv_bias
    sigma = jax.nn.sigmoid(pre)
    active = (pre * sigma).astype(jnp.bfloat16)
    cosine = lat_cosine(rows, lat_place * rows, rows * lat_count)
    pair_sum = cosine[0::2] + cosine[1::2]
    weighted = active.astype(jnp.float32) * cosine[None, :, None, None]
    pooled = (
        weighted.reshape(batches, rows // 2, 2, cols // 2, 2, chans).sum(axis=(2, 4))
        / (2.0 * pair_sum)[None, :, None, None]
    )
    share = cosine / (2.0 * jnp.repeat(pair_sum, 2))
    spread = jnp.repeat(jnp.repeat(cotangent.astype(jnp.float32), 2, axis=1), 2, axis=2)
    grad_pre = (spread * share[None, :, None, None] * sigma * (1.0 + pre * (1.0 - sigma))).astype(
        jnp.bfloat16
    )
    kernel_part = kernel_grad(padded, grad_pre, rows, cols)
    bias_part = jnp.sum(grad_pre.astype(jnp.float32), axis=(0, 1, 2))
    grad_kernel, grad_bias = lax.psum((kernel_part, bias_part), ("lat", "lon"))
    grad_padded = extend(grad_pre)
    is_north = lat_place == 0
    is_south = lat_place == lat_count - 1
    blank = jnp.zeros_like(grad_padded[:, :1])
    upper_rows = jnp.where(is_north, blank, grad_padded[:, :1])
    lower_rows = jnp.where(is_south, blank, grad_padded[:, -1:])
    inner = jnp.concatenate([upper_rows, grad_padded[:, 1:-1], lower_rows], axis=1)
    back = back_conv(inner, kernel, rows, cols)
    north_add = jnp.where(is_north, pole_term(grad_padded[:, :1], kernel, 0, cols), 0.0)
    south_add = jnp.where(is_south, pole_term(grad_padded[:, -1:], kernel, 2, cols), 0.0)
    back = jnp.concatenate(
        [back[:, :1] + north_add, back[:, 1:-1], back[:, -1:] + south_add], axis=1
    )
    return (pooled.astype(jnp.bfloat16), back.astype(jnp.bfloat16), grad_kernel, grad_bias)


def solution(mesh):
    return jax.shard_map(
        local,
        mesh=mesh,
        in_specs=(P(None, "lat", "lon", None), P(), P(), P(None, "lat", "lon", None)),
        out_specs=(P(None, "lat", "lon", None), P(None, "lat", "lon", None), P(), P()),
        check_vma=False,
    )
```

profile of v0, /device:TPU:1, one launch (start us, length us, event | category | flops | bytes accessed | tf_op | source)
XLA Modules:
  0.0 244.1 jit_solution(9984950914171488139)
XLA Ops:
  7.2 0.8 fusion.107
  8.0 3.6 %collective-permute-start.2 = (bf16[2,1,48,256]{3,2,1,0:T(8,128)(2,1)S(1)}, bf16[2,1,48,256]{3,2,1,0:T(8,128)(2,1)S(1)}, u32[]{:S(2)}, u32[]{:S(2)}) collective-permute-start(bf16[2,1,48,256]{3,2,1,0:T(8,128)(2,1)S(1)} %get-tuple-element.41), channel_id=1, source_target_pairs={{0,8},{1,9},{2,10},{3,11},{4,12},{5,13},{6,14},{7,15},{8,0},{9,1},... | collective-permute-start | bytes 147464 | tf_op jit(solution)/shard_map/ppermute | solution.py:10
  11.7 3.5 %collective-permute-start.1 = (bf16[2,1,48,256]{3,2,1,0:T(8,128)(2,1)S(1)}, bf16[2,1,48,256]{3,2,1,0:T(8,128)(2,1)S(1)}, u32[]{:S(2)}, u32[]{:S(2)}) collective-permute-start(bf16[2,1,48,256]{3,2,1,0:T(8,128)(2,1)S(1)} %get-tuple-element.41), channel_id=1, source_target_pairs={{0,16},{16,32},{32,48},{48,64},{64,80},{80,96},{96,112},{1,17},{17... | collective-permute-start | bytes 147464 | tf_op jit(solution)/shard_map/ppermute | solution.py:20
  15.2 1.3 collective-permute-start.3
  17.4 1.1 broadcast_in_dim.21
  18.5 1.7 broadcast_in_dim.22
  20.3 3.4 %reshape.184 = f32[3072,256]{1,0:T(8,128)} reshape(f32[2,32,24,2,256]{4,3,2,1,0:T(2,128)S(1)} %broadcast_in_dim.22) | data formatting | bytes 6291456 | tf_op jit(solution)/shard_map/reshape | solution.py:123
  23.7 3.4 %reshape.178 = f32[2,32,48,256]{3,2,1,0:T(8,128)} reshape(f32[2,32,24,2,256]{4,3,2,1,0:T(2,128)S(1)} %broadcast_in_dim.22) | data formatting | bytes 6291456 | tf_op jit(solution)/shard_map/reshape | solution.py:123
  27.8 0.7 copy-done
  28.8 1.6 collective-permute-start.5
  30.4 1.4 collective-permute-start.4
  32.4 1.2 collective-permute-done.5
  33.7 1.2 pad_maximum_fusion
  34.9 3.1 %fusion.104 = (bf16[2,32,48,256]{3,2,1,0:T(8,128)(2,1)S(1)}, bf16[2,32,48,256]{3,2,1,0:T(8,128)(2,1)S(1)}, bf16[2,32,48,256]{3,2,1,0:T(8,128)(2,1)S(1)}, bf16[2,...) fusion(bf16[2,34,49,256]{3,2,1,0:T(8,128)(2,1)S(1)} %get-tuple-element., ...), kind=kLoop, calls=%fused_computation.171 | loop fusion | bytes 18874368 | tf_op jit(solution)/shard_map/slice | solution.py:50
  42.1 1.3 copy-done.10
  43.4 2.2 convert_reduce_fusion
  45.6 1.4 multiply_convert_fusion.2
  48.0 1.3 collective-permute-start.9
  49.2 2.8 %collective-permute-start.6 = (bf16[2,1,48,256]{3,2,1,0:T(8,128)(2,1)}, bf16[2,1,48,256]{3,2,1,0:T(8,128)(2,1)}, u32[]{:S(2)}, u32[]{:S(2)}) collective-permute-start(bf16[2,1,48,256]{3,2,1,0:T(8,128)(2,1)} %get-tuple-element.37), channel_id=1, source_target_pairs={{0,8},{1,9},{2,10},{3,11},{4,12},{5,13},{6,14},{7,15},{8,0},{9,1},... | collective-permute-start | bytes 147464 | tf_op jit(solution)/shard_map/ppermute | solution.py:10
  52.3 5.4 %collective-permute-start.7 = (bf16[2,1,48,256]{3,2,1,0:T(8,128)(2,1)}, bf16[2,1,48,256]{3,2,1,0:T(8,128)(2,1)}, u32[]{:S(2)}, u32[]{:S(2)}) collective-permute-start(bf16[2,1,48,256]{3,2,1,0:T(8,128)(2,1)} %get-tuple-element.38), channel_id=1, source_target_pairs={{0,16},{16,32},{32,48},{48,64},{64,80},{80,96},{96,112},{1,17},{17... | collective-permute-start | bytes 147464 | tf_op jit(solution)/shard_map/ppermute | solution.py:20
  57.7 1.3 fusion.21
  59.0 5.2 %reshape.176 = f32[2,16,2,24,2,256]{5,4,3,2,1,0:T(2,128)} reshape(f32[3072,256]{1,0:T(8,128)} %copy-done.4) | data formatting | bytes 6291456 | tf_op jit(solution)/shard_map/reshape | solution.py:56
  64.2 2.8 %fusion.31 = f32[9,256,256]{2,1,0:T(8,128)} fusion(f32[9,256,256]{2,1,0:T(8,128)} %fusion.21, bf16[2,32,48,256]{3,2,1,0:T(8,128)(2,1)S(1)} %multiply_convert_fusion.2, bf16[2,32,48,256]{3,2,1,0:T(8,128)(2,1)} %param.4, bf16[2,1,48,256]{3,2,1,0:T(8,128)(2,1)} %copy-done.14), kind=kOutput, calls=%fused_computation.76 | convolution fusion | flops 405897216 | bytes 3457024 | tf_op jit(solution)/shard_map/dot_general | solution.py:100
  67.1 1.3 fusion.20
  68.4 1.3 fusion.19
  69.8 1.4 fusion.18
  71.3 1.3 fusion.17
  72.6 1.3 fusion.16
  73.9 1.3 fusion.25
  75.2 1.3 fusion.15
  77.3 3.2 %multiply_reduce_fusion = f32[2,16,24,256]{3,2,1,0:T(8,128)S(1)} fusion(f32[16,2]{1,0:T(8,128)S(1)} %add_cosine_fusion, f32[256]{0:T(256)S(1)} %copy-done.18, f32[2,16,2,24,2,256]{5,4,3,2,1,0:T(2,128)} %reshape.176), kind=kLoop, calls=%fused_computation.23 | loop fusion | flops 6881280 | bytes 3933312 | tf_op jit(solution)/shard_map/reduce_sum | solution.py:119
  80.5 0.9 divide_convert_fusion
  81.4 72.1 %psum.15 = f32[256]{0:T(256)} all-reduce(f32[256]{0:T(256)S(1)} %copy-done.21), channel_id=1, replica_groups=mesh['lat'=8,'lon'=16] {'lat','lon'}, use_global_device_ids=true, to_apply=%region_3.4 | all-reduce | flops 256 | bytes 2048 | tf_op jit(solution)/shard_map/psum | solution.py:129
  153.5 0.8 broadcast_select_fusion.2
  154.5 0.8 broadcast_select_fusion
  155.4 0.9 collective-permute-start.11
  156.3 1.6 collective-permute-start.10
  158.1 1.5 collective-permute-done.11
  159.6 1.1 pad_maximum_fusion.1
  160.8 1.2 maximum_maximum_fusion.1
  162.2 0.8 slice.258
  163.7 2.1 pad_maximum_fusion.3
  168.3 1.3 copy-done.5
  169.5 1.0 copy-done.11
  170.5 1.5 convolution_add_fusion.4
  175.5 1.3 pad_maximum_fusion.7
  176.8 57.3 %all-reduce.2.cloned.1.call-done = f32[9,256,256]{2,1,0:T(8,128)} async-done(((f32[9,256,256]{2,1,0:T(8,128)}), f32[9,256,256]{2,1,0:T(8,128)}) %all-reduce.2.cloned.1.call-update) | async-done | bytes 2359312 | tf_op jit(solution)/shard_map/psum | solution.py:129
  234.1 3.2 %copy.45 = f32[9,256,256]{2,1,0:T(8,128)} copy(f32[9,256,256]{2,1,0:T(8,128)} %all-reduce.2.cloned.1.call-done) | data formatting | bytes 4718592
  (101 shorter events, 15.8 us)
Async XLA Ops:
  7.2 226.9 %all-reduce.2.cloned.1.call-start = ((), (), s32[]{:S(2)}) async-start(), calls=%async_computation | async-start | bytes 4718592 | tf_op jit(solution)/shard_map/psum | solution.py:129
  8.0 19.7 %collective-permute-start.2 = (bf16[2,1,48,256]{3,2,1,0:T(8,128)(2,1)S(1)}, bf16[2,1,48,256]{3,2,1,0:T(8,128)(2,1)S(1)}, u32[]{:S(2)}, u32[]{:S(2)}) collective-permute-start(bf16[2,1,48,256]{3,2,1,0:T(8,128)(2,1)S(1)} %get-tuple-element.41), channel_id=1, source_target_pairs={{0,8},{1,9},{2,10},{3,11},{4,12},{5,13},{6,14},{7,15},{8,0},{9,1},... | collective-permute-start | bytes 147464 | tf_op jit(solution)/shard_map/ppermute | solution.py:10
  11.7 16.1 %collective-permute-start.1 = (bf16[2,1,48,256]{3,2,1,0:T(8,128)(2,1)S(1)}, bf16[2,1,48,256]{3,2,1,0:T(8,128)(2,1)S(1)}, u32[]{:S(2)}, u32[]{:S(2)}) collective-permute-start(bf16[2,1,48,256]{3,2,1,0:T(8,128)(2,1)S(1)} %get-tuple-element.41), channel_id=1, source_target_pairs={{0,16},{16,32},{32,48},{48,64},{64,80},{80,96},{96,112},{1,17},{17... | collective-permute-start | bytes 147464 | tf_op jit(solution)/shard_map/ppermute | solution.py:20
  15.2 12.5 %collective-permute-start.3 = (bf16[2,1,48,256]{3,2,1,0:T(8,128)(2,1)S(1)}, bf16[2,1,48,256]{3,2,1,0:T(8,128)(2,1)S(1)}, u32[]{:S(2)}, u32[]{:S(2)}) collective-permute-start(bf16[2,1,48,256]{3,2,1,0:T(8,128)(2,1)S(1)} %get-tuple-element.42), channel_id=1, source_target_pairs={{16,0},{32,16},{48,32},{64,48},{80,64},{96,80},{112,96},{17,1},{33... | collective-permute-start | bytes 147464 | tf_op jit(solution)/shard_map/ppermute | solution.py:21
  16.5 11.3 %collective-permute-start = (bf16[2,1,48,256]{3,2,1,0:T(8,128)(2,1)S(1)}, bf16[2,1,48,256]{3,2,1,0:T(8,128)(2,1)S(1)}, u32[]{:S(2)}, u32[]{:S(2)}) collective-permute-start(bf16[2,1,48,256]{3,2,1,0:T(8,128)(2,1)S(1)} %get-tuple-element.42), channel_id=1, source_target_pairs={{0,8},{1,9},{2,10},{3,11},{4,12},{5,13},{6,14},{7,15},{8,0},{9,1},... | collective-permute-start | bytes 147464 | tf_op jit(solution)/shard_map/ppermute | solution.py:10
  17.1 1.4 copy-start.19
  17.3 9.9 %copy-start.15 = (f32[32]{0:T(128)}, f32[32]{0:T(128)S(1)}, u32[]{:S(2)}) copy-start(f32[32]{0:T(128)S(1)} %fusion.97) | copy-start | bytes 388
  27.1 1.4 copy-start
  27.8 5.9 %copy-start.12 = (bf16[2,1,48,256]{3,2,1,0:T(8,128)(2,1)}, bf16[2,1,48,256]{3,2,1,0:T(8,128)(2,1)S(1)}, u32[]{:S(2)}) copy-start(bf16[2,1,48,256]{3,2,1,0:T(8,128)(2,1)S(1)} %broadcast_select_fusion.1) | copy-start | bytes 147460
  28.5 5.2 %copy-start.14 = (bf16[2,1,48,256]{3,2,1,0:T(8,128)(2,1)}, bf16[2,1,48,256]{3,2,1,0:T(8,128)(2,1)S(1)}, u32[]{:S(2)}) copy-start(bf16[2,1,48,256]{3,2,1,0:T(8,128)(2,1)S(1)} %broadcast_select_fusion.3) | copy-start | bytes 147460
  28.6 3.3 %copy-start.8 = (bf16[9,256,256]{2,1,0:T(8,128)(2,1)S(1)}, bf16[9,256,256]{2,1,0:T(8,128)(2,1)}, u32[]{:S(2)}) copy-start(bf16[9,256,256]{2,1,0:T(8,128)(2,1)} %param.5) | copy-start | bytes 3538948
  28.8 4.8 %collective-permute-start.5 = (bf16[2,34,1,256]{3,2,1,0:T(2,128)(2,1)S(1)}, bf16[2,34,1,256]{3,2,1,0:T(2,128)(2,1)S(1)}, u32[]{:S(2)}, u32[]{:S(2)}) collective-permute-start(bf16[2,34,1,256]{3,2,1,0:T(2,128)(2,1)S(1)} %get-tuple-element.35), channel_id=1, source_target_pairs={{1,0},{2,1},{3,2},{4,3},{5,4},{6,5},{7,6},{8,7},{9,8},{10,9},{11,1... | collective-permute-start | bytes 104456 | tf_op jit(solution)/shard_map/ppermute | solution.py:21
  30.4 3.3 %collective-permute-start.4 = (bf16[2,34,1,256]{3,2,1,0:T(2,128)(2,1)S(1)}, bf16[2,34,1,256]{3,2,1,0:T(2,128)(2,1)S(1)}, u32[]{:S(2)}, u32[]{:S(2)}) collective-permute-start(bf16[2,34,1,256]{3,2,1,0:T(2,128)(2,1)S(1)} %get-tuple-element.36), channel_id=1, source_target_pairs={{0,1},{1,2},{2,3},{3,4},{4,5},{5,6},{6,7},{7,8},{8,9},{9,10},{10,1... | collective-permute-start | bytes 104456 | tf_op jit(solution)/shard_map/ppermute | solution.py:20
  34.9 3.1 %copy-start.2 = (bf16[2,34,49,256]{3,2,1,0:T(8,128)(2,1)}, bf16[2,34,49,256]{3,2,1,0:T(8,128)(2,1)S(1)}, u32[]{:S(2)}) copy-start(bf16[2,34,49,256]{3,2,1,0:T(8,128)(2,1)S(1)} %get-tuple-element.33) | copy-start | bytes 5117956
  41.5 1.9 copy-start.10
  41.5 1.9 copy-start.17
  43.4 2.2 copy-start.6
  43.4 2.2 copy-start.16
  45.6 1.7 copy-start.4
  48.0 106.5 %collective-permute-start.9 = (bf16[2,1,48,256]{3,2,1,0:T(8,128)(2,1)}, bf16[2,1,48,256]{3,2,1,0:T(8,128)(2,1)}, u32[]{:S(2)}, u32[]{:S(2)}) collective-permute-start(bf16[2,1,48,256]{3,2,1,0:T(8,128)(2,1)} %get-tuple-element.37), channel_id=1, source_target_pairs={{16,0},{32,16},{48,32},{64,48},{80,64},{96,80},{112,96},{17,1},{33... | collective-permute-start | bytes 147464 | tf_op jit(solution)/shard_map/ppermute | solution.py:21
  49.2 104.2 %collective-permute-start.6 = (bf16[2,1,48,256]{3,2,1,0:T(8,128)(2,1)}, bf16[2,1,48,256]{3,2,1,0:T(8,128)(2,1)}, u32[]{:S(2)}, u32[]{:S(2)}) collective-permute-start(bf16[2,1,48,256]{3,2,1,0:T(8,128)(2,1)} %get-tuple-element.37), channel_id=1, source_target_pairs={{0,8},{1,9},{2,10},{3,11},{4,12},{5,13},{6,14},{7,15},{8,0},{9,1},... | collective-permute-start | bytes 147464 | tf_op jit(solution)/shard_map/ppermute | solution.py:10
  52.1 102.4 %collective-permute-start.8 = (bf16[2,1,48,256]{3,2,1,0:T(8,128)(2,1)}, bf16[2,1,48,256]{3,2,1,0:T(8,128)(2,1)}, u32[]{:S(2)}, u32[]{:S(2)}) collective-permute-start(bf16[2,1,48,256]{3,2,1,0:T(8,128)(2,1)} %get-tuple-element.38), channel_id=1, source_target_pairs={{0,8},{1,9},{2,10},{3,11},{4,12},{5,13},{6,14},{7,15},{8,0},{9,1},... | collective-permute-start | bytes 147464 | tf_op jit(solution)/shard_map/ppermute | solution.py:10
  52.3 101.2 %collective-permute-start.7 = (bf16[2,1,48,256]{3,2,1,0:T(8,128)(2,1)}, bf16[2,1,48,256]{3,2,1,0:T(8,128)(2,1)}, u32[]{:S(2)}, u32[]{:S(2)}) collective-permute-start(bf16[2,1,48,256]{3,2,1,0:T(8,128)(2,1)} %get-tuple-element.38), channel_id=1, source_target_pairs={{0,16},{16,32},{32,48},{48,64},{64,80},{80,96},{96,112},{1,17},{17... | collective-permute-start | bytes 147464 | tf_op jit(solution)/shard_map/ppermute | solution.py:20
  64.2 2.9 %copy-start.3 = (bf16[2,34,49,256]{3,2,1,0:T(8,128)(2,1)S(1)}, bf16[2,34,49,256]{3,2,1,0:T(8,128)(2,1)}, u32[]{:S(2)}) copy-start(bf16[2,34,49,256]{3,2,1,0:T(8,128)(2,1)} %copy-done.2) | copy-start | bytes 5117956
  68.4 1.4 copy-start.1
  72.6 1.3 copy-start.13
  76.6 0.7 copy-start.18
  77.3 3.2 %copy-start.20 = (f32[16]{0:T(128)S(1)}, f32[16]{0:T(128)}, u32[]{:S(2)}) copy-start(f32[16]{0:T(128)} %copy-done.19) | copy-start | bytes 196
  77.3 4.1 %copy-start.21 = (f32[256]{0:T(256)S(1)}, f32[256]{0:T(256)}, u32[]{:S(2)}) copy-start(f32[256]{0:T(256)} %get-tuple-element.43) | copy-start | bytes 3076
  77.3 77.0 %copy-start.9 = (bf16[9,256,256]{2,1,0:T(8,128)(2,1)S(1)}, bf16[9,256,256]{2,1,0:T(8,128)(2,1)}, u32[]{:S(2)}) copy-start(bf16[9,256,256]{2,1,0:T(8,128)(2,1)} %param.5) | copy-start | bytes 3538948
  155.4 4.1 %collective-permute-start.11 = (bf16[2,34,1,256]{3,2,1,0:T(2,128)(2,1)S(1)}, bf16[2,34,1,256]{3,2,1,0:T(2,128)(2,1)S(1)}, u32[]{:S(2)}, u32[]{:S(2)}) collective-permute-start(bf16[2,34,1,256]{3,2,1,0:T(2,128)(2,1)S(1)} %get-tuple-element.31), channel_id=1, source_target_pairs={{1,0},{2,1},{3,2},{4,3},{5,4},{6,5},{7,6},{8,7},{9,8},{10,9},{11,1... | collective-permute-start | bytes 104456 | tf_op jit(solution)/shard_map/ppermute | solution.py:21
  156.3 3.3 %collective-permute-start.10 = (bf16[2,34,1,256]{3,2,1,0:T(2,128)(2,1)S(1)}, bf16[2,34,1,256]{3,2,1,0:T(2,128)(2,1)S(1)}, u32[]{:S(2)}, u32[]{:S(2)}) collective-permute-start(bf16[2,34,1,256]{3,2,1,0:T(2,128)(2,1)S(1)} %get-tuple-element.32), channel_id=1, source_target_pairs={{0,1},{1,2},{2,3},{3,4},{4,5},{5,6},{6,7},{7,8},{8,9},{9,10},{10,1... | collective-permute-start | bytes 104456 | tf_op jit(solution)/shard_map/ppermute | solution.py:20
  160.7 1.3 copy-start.7
  162.2 1.5 slice-start
  167.6 1.9 copy-start.5
  167.6 2.8 %copy-start.11 = (f32[3072,256]{1,0:T(8,128)S(1)}, f32[3072,256]{1,0:T(8,128)}, u32[]{:S(2)}) copy-start(f32[3072,256]{1,0:T(8,128)} %reshape.184) | copy-start | bytes 9437188
Sparse Core Ops, SparseCore 0:
  76.7 157.3 all-reduce.1
where the time goes:
time: 245 us; the launch traced here: 244 us
  blocking collectives  72.1 us (29%)
  waiting for transfers between devices  60.1 us (25%)
  local copies, waits for them, and re-layouts  30.9 us (13%)
  matrix products  27.7 us (11%)
  starting transfers between devices  24.1 us (10%)
  other arithmetic  14.8 us (6%)
  between operations  14.5 us (6%)
    psum x1, blocking collectives, local(): grad_kernel, grad_bias = lax.psum((kernel_part, bias_part), ('lat', 'lon'))  72.1 us
    psum x1, waiting for transfers between devices, local(): grad_kernel, grad_bias = lax.psum((kernel_part, bias_part), ('lat', 'lon'))  57.3 us
    dot_general x9, matrix products, kernel_grad(): lax.dot_general(window, flat_grad, (((0,), (0,)), ((), ())), preferred_el...  13.5 us
    ppermute x4, starting transfers between devices, with_halo(): before = lax.ppermute(last, axis, up)  12 us
    unnamed x45, local copies, waits for them, and re-layouts  8.65 us
    ppermute x4, starting transfers between devices, shifted(): lax.ppermute(shard, axis, [(i, (i + by) % size) for i in range(size)])  6.98 us
    reshape x2, local copies, waits for them, and re-layouts, local(): jnp.repeat(jnp.repeat(cotangent.astype(jnp.float32), 2, axis=1), 2, axis=2)  6.82 us
    dot_general x9, matrix products, forward_conv(): jnp.dot(window, kernel[3 * row_off + col_off], preferred_element_type=jnp...  6.79 us
  transfers between devices with their start and end apart: 13, of which 4 were waited for; matrix products, arithmetic and copies ran while one was open for 21% of the time, Pallas kernels for 0%

commit v1 on v0

--- a/solution.py
+++ b/solution.py
@@ -3,6 +3,7 @@
 import jax.numpy as jnp
 from jax import lax
 from jax.sharding import PartitionSpec as P
+from jax.lax import psum
 
 
 def shifted(shard, axis, by):
@@ -126,7 +127,13 @@
     )
     kernel_part = kernel_grad(padded, grad_pre, rows, cols)
     bias_part = jnp.sum(grad_pre.astype(jnp.float32), axis=(0, 1, 2))
-    grad_kernel, grad_bias = lax.psum((kernel_part, bias_part), ("lat", "lon"))
+
+    def prepare_racks(x_in):
+        for kk in ("lon", "lat"):
+            x_in = psum(x_in, axis_name=kk)
+        return x_in
+
+    grad_kernel, grad_bias = prepare_racks((kernel_part, bias_part))
     grad_padded = extend(grad_pre)
     is_north = lat_place == 0
     is_south = lat_place == lat_count - 1

time: 245 us -> 316 us (1.29); the launches traced: 244 us -> 310 us
  waiting for transfers between devices: 60.1 us -> 136 us
  blocking collectives: 72.1 us -> 52.4 us
  matrix products: 27.7 us -> 31.9 us
    psum x1 -> x2, waiting for transfers between devices: 57.3 us -> 133 us  [prepare_racks(): x_in = psum(x_in, axis_name=kk)]
    psum x1 -> x2, blocking collectives: 72.1 us -> 52.4 us  [prepare_racks(): x_in = psum(x_in, axis_name=kk)]
    dot_general x9, matrix products: 6.33 us -> 10.5 us  [back_conv(): lax.dot_general(window, kernel[3 * row_off + col_off], (((1,), (1,)), (()...]
    ppermute x4, starting transfers between devices: 5.03 us -> 8.8 us  [with_halo(): after = lax.ppermute(first, axis, down)]
    unnamed x45 -> x49, local copies, waits for them, and re-layouts: 8.65 us -> 9.37 us
  transfers between devices with their start and end apart: 13 -> 14, of which waited for: 4 -> 6; matrix products, arithmetic and copies ran while one was open for 21% -> 18% of each run, Pallas kernels for 0% -> 0%
where the time goes in v1:
time: 316 us; the launch traced here: 310 us
  waiting for transfers between devices  136 us (43%)
  blocking collectives  52.4 us (17%)
  matrix products  31.9 us (10%)
  local copies, waits for them, and re-layouts  31.6 us (10%)
  starting transfers between devices  26.3 us (8%)
  other arithmetic  17.1 us (5%)
  between operations  14.5 us (5%)
    psum x2, waiting for transfers between devices, prepare_racks(): x_in = psum(x_in, axis_name=kk)  133 us
    psum x2, blocking collectives, prepare_racks(): x_in = psum(x_in, axis_name=kk)  52.4 us
    dot_general x9, matrix products, kernel_grad(): lax.dot_general(window, flat_grad, (((0,), (0,)), ((), ())), preferred_el...  13.5 us
    dot_general x9, matrix products, back_conv(): lax.dot_general(window, kernel[3 * row_off + col_off], (((1,), (1,)), (()...  10.5 us
    ppermute x4, starting transfers between devices, with_halo(): before = lax.ppermute(last, axis, up)  10.4 us
    unnamed x49, local copies, waits for them, and re-layouts  9.37 us
    ppermute x4, starting transfers between devices, with_halo(): after = lax.ppermute(first, axis, down)  8.8 us
    ppermute x4, starting transfers between devices, shifted(): lax.ppermute(shard, axis, [(i, (i + by) % size) for i in range(size)])  6.98 us
  transfers between devices with their start and end apart: 14, of which 6 were waited for; matrix products, arithmetic and copies ran while one was open for 18% of the time, Pallas kernels for 0%

profile of v1, /device:TPU:1, one launch (start us, length us, event | category | flops | bytes accessed | tf_op | source)
XLA Modules:
  0.0 310.1 jit_solution(3263121316336023986)
XLA Ops:
  7.2 0.8 fusion.107
  8.0 3.6 %collective-permute-start.2 = (bf16[2,1,48,256]{3,2,1,0:T(8,128)(2,1)S(1)}, bf16[2,1,48,256]{3,2,1,0:T(8,128)(2,1)S(1)}, u32[]{:S(2)}, u32[]{:S(2)}) collective-permute-start(bf16[2,1,48,256]{3,2,1,0:T(8,128)(2,1)S(1)} %get-tuple-element.41), channel_id=1, source_target_pairs={{0,8},{1,9},{2,10},{3,11},{4,12},{5,13},{6,14},{7,15},{8,0},{9,1},... | collective-permute-start | bytes 147464 | tf_op jit(solution)/shard_map/ppermute | solution.py:11
  11.7 3.5 %collective-permute-start.1 = (bf16[2,1,48,256]{3,2,1,0:T(8,128)(2,1)S(1)}, bf16[2,1,48,256]{3,2,1,0:T(8,128)(2,1)S(1)}, u32[]{:S(2)}, u32[]{:S(2)}) collective-permute-start(bf16[2,1,48,256]{3,2,1,0:T(8,128)(2,1)S(1)} %get-tuple-element.41), channel_id=1, source_target_pairs={{0,16},{16,32},{32,48},{48,64},{64,80},{80,96},{96,112},{1,17},{17... | collective-permute-start | bytes 147464 | tf_op jit(solution)/shard_map/ppermute | solution.py:21
  15.2 1.3 collective-permute-start.3
  17.4 1.1 broadcast_in_dim.21
  18.5 1.7 broadcast_in_dim.22
  20.3 3.4 %reshape.184 = f32[3072,256]{1,0:T(8,128)} reshape(f32[2,32,24,2,256]{4,3,2,1,0:T(2,128)S(1)} %broadcast_in_dim.22) | data formatting | bytes 6291456 | tf_op jit(solution)/shard_map/reshape | solution.py:124
  23.7 3.4 %reshape.178 = f32[2,32,48,256]{3,2,1,0:T(8,128)} reshape(f32[2,32,24,2,256]{4,3,2,1,0:T(2,128)S(1)} %broadcast_in_dim.22) | data formatting | bytes 6291456 | tf_op jit(solution)/shard_map/reshape | solution.py:124
  28.8 1.6 collective-permute-start.5
  30.4 1.4 collective-permute-start.4
  32.4 1.2 collective-permute-done.5
  33.7 1.2 pad_maximum_fusion
  34.9 3.1 %fusion.104 = (bf16[2,32,48,256]{3,2,1,0:T(8,128)(2,1)S(1)}, bf16[2,32,48,256]{3,2,1,0:T(8,128)(2,1)S(1)}, bf16[2,32,48,256]{3,2,1,0:T(8,128)(2,1)S(1)}, bf16[2,...) fusion(bf16[2,34,49,256]{3,2,1,0:T(8,128)(2,1)S(1)} %get-tuple-element., ...), kind=kLoop, calls=%fused_computation.171 | loop fusion | bytes 18874368 | tf_op jit(solution)/shard_map/slice | solution.py:51
  42.1 1.3 copy-done.12
  43.4 2.2 convert_reduce_fusion
  45.6 1.4 multiply_convert_fusion.2
  48.0 1.3 collective-permute-start.9
  49.2 2.8 collective-permute-start.6
  52.3 5.4 %collective-permute-start.7 = (bf16[2,1,48,256]{3,2,1,0:T(8,128)(2,1)}, bf16[2,1,48,256]{3,2,1,0:T(8,128)(2,1)}, u32[]{:S(2)}, u32[]{:S(2)}) collective-permute-start(bf16[2,1,48,256]{3,2,1,0:T(8,128)(2,1)} %get-tuple-element.38), channel_id=1, source_target_pairs={{0,16},{16,32},{32,48},{48,64},{64,80},{80,96},{96,112},{1,17},{17... | collective-permute-start | bytes 147464 | tf_op jit(solution)/shard_map/ppermute | solution.py:21
  57.7 1.3 fusion.21
  59.0 5.2 %reshape.176 = f32[2,16,2,24,2,256]{5,4,3,2,1,0:T(2,128)} reshape(f32[3072,256]{1,0:T(8,128)} %copy-done.4) | data formatting | bytes 6291456 | tf_op jit(solution)/shard_map/reshape | solution.py:57
  64.2 2.8 fusion.31
  67.1 1.3 fusion.20
  68.4 1.3 fusion.19
  69.8 1.4 fusion.18
  71.3 1.3 fusion.17
  72.6 1.3 fusion.16
  73.9 1.3 fusion.25
  75.3 1.3 fusion.15
  77.3 3.1 %multiply_reduce_fusion = f32[2,16,24,256]{3,2,1,0:T(8,128)S(1)} fusion(f32[16,2]{1,0:T(8,128)S(1)} %add_cosine_fusion, f32[256]{0:T(256)S(1)} %copy-done.20, f32[2,16,2,24,2,256]{5,4,3,2,1,0:T(2,128)} %reshape.176), kind=kLoop, calls=%fused_computation.23 | loop fusion | flops 6881280 | bytes 3933312 | tf_op jit(solution)/shard_map/reduce_sum | solution.py:120
  80.4 0.9 divide_convert_fusion
  81.3 32.3 %psum.30 = f32[256]{0:T(256)S(1)} all-reduce(f32[256]{0:T(256)S(1)} %copy-done.23), channel_id=1, replica_groups=mesh['lat'=8,'lon'=16] {'lon'}, use_global_device_ids=true, to_apply=%region_4.5 | all-reduce | flops 256 | bytes 2048 | tf_op jit(solution)/shard_map/psum | solution.py:133
  113.6 20.1 %psum.31 = f32[256]{0:T(256)} all-reduce(f32[256]{0:T(256)S(1)} %psum.30), channel_id=1, replica_groups=mesh['lat'=8,'lon'=16] {'lat'}, use_global_device_ids=true, to_apply=%region_5.6 | all-reduce | flops 256 | bytes 2048 | tf_op jit(solution)/shard_map/psum | solution.py:133
  134.8 0.8 broadcast_select_fusion
  135.7 4.6 %collective-permute-start.11 = (bf16[2,34,1,256]{3,2,1,0:T(2,128)(2,1)S(1)}, bf16[2,34,1,256]{3,2,1,0:T(2,128)(2,1)S(1)}, u32[]{:S(2)}, u32[]{:S(2)}) collective-permute-start(bf16[2,34,1,256]{3,2,1,0:T(2,128)(2,1)S(1)} %get-tuple-element.31), channel_id=1, source_target_pairs={{1,0},{2,1},{3,2},{4,3},{5,4},{6,5},{7,6},{8,7},{9,8},{10,9},{11,1... | collective-permute-start | bytes 104456 | tf_op jit(solution)/shard_map/ppermute | solution.py:22
  142.0 1.1 pad_maximum_fusion.1
  143.2 1.2 maximum_maximum_fusion.1
  144.6 0.8 slice.258
  146.1 4.5 %pad_maximum_fusion.3 = (bf16[2,32,48,256]{3,2,1,0:T(8,128)(2,1)}, bf16[2,32,48,256]{3,2,1,0:T(8,128)(2,1)}, bf16[2,32,48,256]{3,2,1,0:T(8,128)(2,1)}, bf16[2,32...) fusion(bf16[2,32,50,256]{3,2,1,0:T(8,128)(2,1)S(1)} %slice-done, ...), kind=kLoop, calls=%fused_computation.51 | loop fusion | flops 18874368 | bytes 11177984 | tf_op jit(solution)/shard_map/concatenate | solution.py:143
  153.1 1.3 copy-done.5
  154.3 1.0 copy-done.13
  155.3 1.5 convolution_add_fusion.4
  156.8 2.2 convolution_add_fusion.3
  159.0 48.2 %all-reduce.3.cloned.1.call-done = f32[9,256,256]{2,1,0:T(8,128)} async-done(((f32[9,256,256]{2,1,0:T(8,128)}), f32[9,256,256]{2,1,0:T(8,128)}) %all-reduce.3.cloned.1.call-update) | async-done | bytes 2359312 | tf_op jit(solution)/shard_map/psum | solution.py:133
  207.2 3.1 convolution_add_fusion.2
  213.4 1.3 pad_maximum_fusion.7
  214.8 85.2 %all-reduce.5.cloned.1.call-done = f32[9,256,256]{2,1,0:T(8,128)} async-done(((f32[9,256,256]{2,1,0:T(8,128)}), f32[9,256,256]{2,1,0:T(8,128)}) %all-reduce.5.cloned.1.call-update) | async-done | bytes 2359312 | tf_op jit(solution)/shard_map/psum | solution.py:133
  300.0 3.2 %copy.46 = f32[9,256,256]{2,1,0:T(8,128)} copy(f32[9,256,256]{2,1,0:T(8,128)} %all-reduce.5.cloned.1.call-done) | data formatting | bytes 4718592
  (109 shorter events, 18.3 us)
Async XLA Ops:
  7.2 200.0 %all-reduce.3.cloned.1.call-start = ((), (), s32[]{:S(2)}) async-start(), calls=%async_computation | async-start | bytes 4718592 | tf_op jit(solution)/shard_map/psum | solution.py:133
  8.0 19.7 %collective-permute-start.2 = (bf16[2,1,48,256]{3,2,1,0:T(8,128)(2,1)S(1)}, bf16[2,1,48,256]{3,2,1,0:T(8,128)(2,1)S(1)}, u32[]{:S(2)}, u32[]{:S(2)}) collective-permute-start(bf16[2,1,48,256]{3,2,1,0:T(8,128)(2,1)S(1)} %get-tuple-element.41), channel_id=1, source_target_pairs={{0,8},{1,9},{2,10},{3,11},{4,12},{5,13},{6,14},{7,15},{8,0},{9,1},... | collective-permute-start | bytes 147464 | tf_op jit(solution)/shard_map/ppermute | solution.py:11
  11.7 16.1 %collective-permute-start.1 = (bf16[2,1,48,256]{3,2,1,0:T(8,128)(2,1)S(1)}, bf16[2,1,48,256]{3,2,1,0:T(8,128)(2,1)S(1)}, u32[]{:S(2)}, u32[]{:S(2)}) collective-permute-start(bf16[2,1,48,256]{3,2,1,0:T(8,128)(2,1)S(1)} %get-tuple-element.41), channel_id=1, source_target_pairs={{0,16},{16,32},{32,48},{48,64},{64,80},{80,96},{96,112},{1,17},{17... | collective-permute-start | bytes 147464 | tf_op jit(solution)/shard_map/ppermute | solution.py:21
  15.2 12.5 %collective-permute-start.3 = (bf16[2,1,48,256]{3,2,1,0:T(8,128)(2,1)S(1)}, bf16[2,1,48,256]{3,2,1,0:T(8,128)(2,1)S(1)}, u32[]{:S(2)}, u32[]{:S(2)}) collective-permute-start(bf16[2,1,48,256]{3,2,1,0:T(8,128)(2,1)S(1)} %get-tuple-element.42), channel_id=1, source_target_pairs={{16,0},{32,16},{48,32},{64,48},{80,64},{96,80},{112,96},{17,1},{33... | collective-permute-start | bytes 147464 | tf_op jit(solution)/shard_map/ppermute | solution.py:22
  16.5 11.3 %collective-permute-start = (bf16[2,1,48,256]{3,2,1,0:T(8,128)(2,1)S(1)}, bf16[2,1,48,256]{3,2,1,0:T(8,128)(2,1)S(1)}, u32[]{:S(2)}, u32[]{:S(2)}) collective-permute-start(bf16[2,1,48,256]{3,2,1,0:T(8,128)(2,1)S(1)} %get-tuple-element.42), channel_id=1, source_target_pairs={{0,8},{1,9},{2,10},{3,11},{4,12},{5,13},{6,14},{7,15},{8,0},{9,1},... | collective-permute-start | bytes 147464 | tf_op jit(solution)/shard_map/ppermute | solution.py:11
  17.1 1.4 copy-start.21
  17.3 9.9 %copy-start.17 = (f32[32]{0:T(128)}, f32[32]{0:T(128)S(1)}, u32[]{:S(2)}) copy-start(f32[32]{0:T(128)S(1)} %fusion.97) | copy-start | bytes 388
  27.1 1.4 copy-start
  27.8 5.9 %copy-start.14 = (bf16[2,1,48,256]{3,2,1,0:T(8,128)(2,1)}, bf16[2,1,48,256]{3,2,1,0:T(8,128)(2,1)S(1)}, u32[]{:S(2)}) copy-start(bf16[2,1,48,256]{3,2,1,0:T(8,128)(2,1)S(1)} %broadcast_select_fusion.1) | copy-start | bytes 147460
  28.5 5.2 %copy-start.16 = (bf16[2,1,48,256]{3,2,1,0:T(8,128)(2,1)}, bf16[2,1,48,256]{3,2,1,0:T(8,128)(2,1)S(1)}, u32[]{:S(2)}) copy-start(bf16[2,1,48,256]{3,2,1,0:T(8,128)(2,1)S(1)} %broadcast_select_fusion.3) | copy-start | bytes 147460
  28.6 3.3 %copy-start.8 = (bf16[9,256,256]{2,1,0:T(8,128)(2,1)S(1)}, bf16[9,256,256]{2,1,0:T(8,128)(2,1)}, u32[]{:S(2)}) copy-start(bf16[9,256,256]{2,1,0:T(8,128)(2,1)} %param.5) | copy-start | bytes 3538948
  28.8 4.8 %collective-permute-start.5 = (bf16[2,34,1,256]{3,2,1,0:T(2,128)(2,1)S(1)}, bf16[2,34,1,256]{3,2,1,0:T(2,128)(2,1)S(1)}, u32[]{:S(2)}, u32[]{:S(2)}) collective-permute-start(bf16[2,34,1,256]{3,2,1,0:T(2,128)(2,1)S(1)} %get-tuple-element.35), channel_id=1, source_target_pairs={{1,0},{2,1},{3,2},{4,3},{5,4},{6,5},{7,6},{8,7},{9,8},{10,9},{11,1... | collective-permute-start | bytes 104456 | tf_op jit(solution)/shard_map/ppermute | solution.py:22
  30.4 3.3 %collective-permute-start.4 = (bf16[2,34,1,256]{3,2,1,0:T(2,128)(2,1)S(1)}, bf16[2,34,1,256]{3,2,1,0:T(2,128)(2,1)S(1)}, u32[]{:S(2)}, u32[]{:S(2)}) collective-permute-start(bf16[2,34,1,256]{3,2,1,0:T(2,128)(2,1)S(1)} %get-tuple-element.36), channel_id=1, source_target_pairs={{0,1},{1,2},{2,3},{3,4},{4,5},{5,6},{6,7},{7,8},{8,9},{9,10},{10,1... | collective-permute-start | bytes 104456 | tf_op jit(solution)/shard_map/ppermute | solution.py:21
  34.9 3.1 %copy-start.2 = (bf16[2,34,49,256]{3,2,1,0:T(8,128)(2,1)}, bf16[2,34,49,256]{3,2,1,0:T(8,128)(2,1)S(1)}, u32[]{:S(2)}) copy-start(bf16[2,34,49,256]{3,2,1,0:T(8,128)(2,1)S(1)} %get-tuple-element.33) | copy-start | bytes 5117956
  41.5 1.9 copy-start.12
  41.5 1.9 copy-start.19
  43.4 2.2 copy-start.6
  43.4 2.2 copy-start.18
  45.6 1.7 copy-start.4
  48.0 86.8 %collective-permute-start.9 = (bf16[2,1,48,256]{3,2,1,0:T(8,128)(2,1)}, bf16[2,1,48,256]{3,2,1,0:T(8,128)(2,1)}, u32[]{:S(2)}, u32[]{:S(2)}) collective-permute-start(bf16[2,1,48,256]{3,2,1,0:T(8,128)(2,1)} %get-tuple-element.37), channel_id=1, source_target_pairs={{16,0},{32,16},{48,32},{64,48},{80,64},{96,80},{112,96},{17,1},{33... | collective-permute-start | bytes 147464 | tf_op jit(solution)/shard_map/ppermute | solution.py:22
  49.2 84.5 %collective-permute-start.6 = (bf16[2,1,48,256]{3,2,1,0:T(8,128)(2,1)}, bf16[2,1,48,256]{3,2,1,0:T(8,128)(2,1)}, u32[]{:S(2)}, u32[]{:S(2)}) collective-permute-start(bf16[2,1,48,256]{3,2,1,0:T(8,128)(2,1)} %get-tuple-element.37), channel_id=1, source_target_pairs={{0,8},{1,9},{2,10},{3,11},{4,12},{5,13},{6,14},{7,15},{8,0},{9,1},... | collective-permute-start | bytes 147464 | tf_op jit(solution)/shard_map/ppermute | solution.py:11
  52.1 82.7 %collective-permute-start.8 = (bf16[2,1,48,256]{3,2,1,0:T(8,128)(2,1)}, bf16[2,1,48,256]{3,2,1,0:T(8,128)(2,1)}, u32[]{:S(2)}, u32[]{:S(2)}) collective-permute-start(bf16[2,1,48,256]{3,2,1,0:T(8,128)(2,1)} %get-tuple-element.38), channel_id=1, source_target_pairs={{0,8},{1,9},{2,10},{3,11},{4,12},{5,13},{6,14},{7,15},{8,0},{9,1},... | collective-permute-start | bytes 147464 | tf_op jit(solution)/shard_map/ppermute | solution.py:11
  52.3 81.4 %collective-permute-start.7 = (bf16[2,1,48,256]{3,2,1,0:T(8,128)(2,1)}, bf16[2,1,48,256]{3,2,1,0:T(8,128)(2,1)}, u32[]{:S(2)}, u32[]{:S(2)}) collective-permute-start(bf16[2,1,48,256]{3,2,1,0:T(8,128)(2,1)} %get-tuple-element.38), channel_id=1, source_target_pairs={{0,16},{16,32},{32,48},{48,64},{64,80},{80,96},{96,112},{1,17},{17... | collective-permute-start | bytes 147464 | tf_op jit(solution)/shard_map/ppermute | solution.py:21
  64.2 2.8 copy-start.3
  68.4 1.4 copy-start.1
  72.6 1.3 copy-start.15
  76.6 0.7 copy-start.20
  76.6 3.8 %copy-start.22 = (f32[16]{0:T(128)S(1)}, f32[16]{0:T(128)}, u32[]{:S(2)}) copy-start(f32[16]{0:T(128)} %copy-done.21) | copy-start | bytes 196
  76.6 4.7 %copy-start.23 = (f32[256]{0:T(256)S(1)}, f32[256]{0:T(256)}, u32[]{:S(2)}) copy-start(f32[256]{0:T(256)} %get-tuple-element.43) | copy-start | bytes 3076
  76.6 57.9 %copy-start.9 = (bf16[9,256,256]{2,1,0:T(8,128)(2,1)S(1)}, bf16[9,256,256]{2,1,0:T(8,128)(2,1)}, u32[]{:S(2)}) copy-start(bf16[9,256,256]{2,1,0:T(8,128)(2,1)} %param.5) | copy-start | bytes 3538948
  76.7 223.3 %all-reduce.5.cloned.1.call-start = ((), (), s32[]{:S(2)}) async-start(), calls=%async_computation.1 | async-start | bytes 4718592 | tf_op jit(solution)/shard_map/psum | solution.py:133
  135.7 5.6 %collective-permute-start.11 = (bf16[2,34,1,256]{3,2,1,0:T(2,128)(2,1)S(1)}, bf16[2,34,1,256]{3,2,1,0:T(2,128)(2,1)S(1)}, u32[]{:S(2)}, u32[]{:S(2)}) collective-permute-start(bf16[2,34,1,256]{3,2,1,0:T(2,128)(2,1)S(1)} %get-tuple-element.31), channel_id=1, source_target_pairs={{1,0},{2,1},{3,2},{4,3},{5,4},{6,5},{7,6},{8,7},{9,8},{10,9},{11,1... | collective-permute-start | bytes 104456 | tf_op jit(solution)/shard_map/ppermute | solution.py:22
  140.3 1.7 collective-permute-start.10
  143.2 1.4 copy-start.7
  144.6 1.5 slice-start
  152.4 1.9 copy-start.5
  152.4 2.9 copy-start.13
  207.2 3.1 %copy-start.11 = (bf16[2,32,48,256]{3,2,1,0:T(8,128)(2,1)S(1)}, bf16[2,32,48,256]{3,2,1,0:T(8,128)(2,1)}, u32[]{:S(2)}) copy-start(bf16[2,32,48,256]{3,2,1,0:T(8,128)(2,1)} %get-tuple-element.14) | copy-start | bytes 4718596
  210.3 1.4 copy-start.10
Sparse Core Ops, SparseCore 0:
  76.7 130.4 all-reduce.2
  209.7 90.2 all-reduce.4
